TPU v7x, 32 devices: a whole 2x2x4 slice. The times are simulated.
32 devices in a mesh: src: 4 (over y, core), dst: 8 (over z, x).
Axes of the slice: x: 2, y: 2, z: 4, core: 2. Of those that a mesh axis runs over, the one named last changes fastest.
Arguments:
- features: bfloat16 [8192, 768], P(('src', 'dst')), may hold values from -6 to 6
- edge_tiles: bfloat16 [4, 8, 64, 128, 128], P('src', 'dst'), may hold values from -0.3125 to 0.3125
- tile_src: int32 [4, 8, 64], P('src', 'dst'), may hold values from 0 to 7
- tile_dst: int32 [4, 8, 64], P('src', 'dst'), may hold values from 0 to 15, as said below
- tile_count: int32 [4, 8], P('src', 'dst'), may hold values from 1 to 64, as said below
- weight: bfloat16 [768, 1024], replicated, may hold values from -0.21875 to 0.21875
- out_bias: float32 [1024], replicated, may hold values from -3 to 3
- out_grad: bfloat16 [8192, 1024], P(('src', 'dst')), may hold values from -6 to 6
Outputs:
- hidden: bfloat16 [8192, 1024], P(('src', 'dst'))
- feature_grad: bfloat16 [8192, 768], P(('src', 'dst'))
- weight_grad: float32 [768, 1024], replicated
- bias_grad: float32 [1024], replicated
Inputs may be any that keep to these rules, and one draw needn't show every extreme that they name: `tile_src`: block s of the source column of device (i, k) is block s % 2 of device (s // 2, k). `tile_dst`: block e of the destination row of device (i, k) is block e % 2 of device (i, e // 2). On one device, all tile slots whose destination blocks lie on one device name the same block. In every row of devices, slot 0 of every device names one common block. `tile_count`: some device uses all 64 slots.
All inputs are finite; a program needn't handle non-finite values.
Results may differ from a plain program's by a relative error of at most 0.024.
Values may be sent and summed in bfloat16 or wider, within the bound.
A program may use at most 128 MiB of HBM per device.

v0:
```python
import jax
import jax.numpy as jnp
from jax import lax
from jax.sharding import PartitionSpec as P


def per_device(features, edge_tiles, tile_src, tile_dst, tile_count, weight, out_bias, out_grad):
    capacity = edge_tiles.shape[2]
    edge_size = edge_tiles.shape[3]
    feat_width = features.shape[1]
    block_rows = features.shape[0]
    blocks = block_rows // edge_size
    masters = lax.axis_size("dst")
    holders = lax.axis_size("src")
    adjacency = edge_tiles.reshape(capacity, edge_size, edge_size)
    src_ids = tile_src.reshape(capacity)
    dst_ids = tile_dst.reshape(capacity)
    tile_total = tile_count.reshape(())
    alive_mask = jnp.arange(capacity, dtype=jnp.int32) < tile_total
    block_ids = jnp.arange(blocks, dtype=jnp.int32)
    owner_ids = dst_ids // blocks
    inner_ids = dst_ids % blocks
    column = lax.all_gather(features, "src", axis=0, tiled=True).reshape(
        holders * blocks, edge_size, feat_width
    )
    picked = column[src_ids]
    partial_value = jnp.einsum(
        "tij,tjf->tif", adjacency, picked, preferred_element_type=jnp.float32
    )
    routing = (owner_ids[None, :] == jnp.arange(masters, dtype=jnp.int32)[:, None]) & alive_mask[
        None, :
    ]
    outgoing = jnp.einsum("pt,tif->pif", routing.astype(jnp.float32), partial_value)
    wanted_block = jnp.max(jnp.where(routing, inner_ids[None, :], 0), axis=1)
    wanted_rows = jnp.broadcast_to(wanted_block[:, None], (masters, edge_size))
    incoming = lax.all_to_all(
        outgoing.astype(jnp.bfloat16), "dst", split_axis=0, concat_axis=0, tiled=True
    )
    asked = lax.all_to_all(wanted_rows, "dst", split_axis=0, concat_axis=0, tiled=True)
    chooser = (asked[None, :, :] == block_ids[:, None, None]).astype(jnp.bfloat16)
    aggregate = jnp.einsum(
        "jpr,prf->jrf", chooser, incoming, preferred_element_type=jnp.float32
    ).astype(jnp.bfloat16)
    preact = (
        jnp.einsum("jrf,fh->jrh", aggregate, weight, preferred_element_type=jnp.float32) + out_bias
    )
    aggregate, preact, asked = (aggregate, preact, asked)
    gate_value = jax.nn.sigmoid(preact)
    hidden = (preact * gate_value).astype(jnp.bfloat16).reshape(block_rows, -1)
    grad_in = out_grad.reshape(blocks, edge_size, -1).astype(jnp.float32)
    pre_grad = grad_in * (gate_value * (1.0 + preact * (1.0 - gate_value)))
    pre_grad_b = pre_grad.astype(jnp.bfloat16)
    weight_term = jnp.einsum(
        "jrf,jrh->fh", aggregate, pre_grad_b, preferred_element_type=jnp.float32
    )
    bias_term = jnp.sum(pre_grad, axis=(0, 1))
    weight_grad, bias_grad = lax.psum((weight_term, bias_term), ("src", "dst"))
    back = jnp.einsum("jrh,fh->jrf", pre_grad_b, weight, preferred_element_type=jnp.float32).astype(
        jnp.bfloat16
    )
    asked_block = asked[:, 0]
    selector = (asked_block[:, None] == block_ids[None, :]).astype(jnp.bfloat16)
    replies = jnp.einsum("pj,jrf->prf", selector, back, preferred_element_type=jnp.float32).astype(
        jnp.bfloat16
    )
    returned = lax.all_to_all(replies, "dst", split_axis=0, concat_axis=0, tiled=True)
    wanted = returned[owner_ids]
    source = jnp.einsum("tji,tjf->tif", adjacency, wanted, preferred_element_type=jnp.float32)
    src_routing = (
        src_ids[None, :] == jnp.arange(holders * blocks, dtype=jnp.int32)[:, None]
    ) & alive_mask[None, :]
    src_terms = jnp.einsum("kt,tif->kif", src_routing.astype(jnp.float32), source)
    summed = lax.psum_scatter(
        src_terms.reshape(holders * block_rows, feat_width).astype(jnp.bfloat16),
        "src",
        scatter_dimension=0,
        tiled=True,
    )
    return (hidden, summed, weight_grad, bias_grad)


def solution(mesh):
    in_specs = (
        P(("src", "dst"), None),
        P("src", "dst", None, None, None),
        P("src", "dst", None),
        P("src", "dst", None),
        P("src", "dst"),
        P(),
        P(),
        P(("src", "dst"), None),
    )
    out_specs = (P(("src", "dst"), None), P(("src", "dst"), None), P(), P())
    return jax.shard_map(
        per_device, mesh=mesh, in_specs=in_specs, out_specs=out_specs, check_vma=False
    )
```

profile of v0, /device:TPU:0, one launch (start us, length us, event | category | flops | bytes accessed | tf_op | source)
XLA Modules:
  0.0 330.1 jit_solution(10724298226550727925)
XLA Ops:
  7.2 0.7 all-gather.2.cloned.1.call-update
  8.6 0.7 and_select_fusion.1
  9.4 0.7 broadcast_in_dim.16
  10.0 7.3 %all-to-all-start.1 = ((s32[8,1,128]{2,1,0:T(1,128)}), s32[8,1,128]{2,1,0:T(1,128)S(1)}, u32[]{:S(2)}, u32[]{:S(2)}) async-start(s32[8,1,128]{2,1,0:T(1,128)} %broadcast_in_dim.16), calls=%async_computation.1 | async-start | bytes 8192 | tf_op jit(solution)/shard_map/all_to_all | solution.py:39
  17.3 0.7 fusion.39
  18.0 14.0 %all-gather.2.cloned.1.call-done = bf16[1024,768]{1,0:T(8,128)(2,1)} async-done(((bf16[256,768]{1,0:T(8,128)(2,1)}), bf16[1024,768]{1,0:T(8,128)(2,1)}) %all-gather.2.cloned.1.call-update) | async-done | bytes 1572880 | tf_op jit(solution)/shard_map/all_gather | solution.py:23
  31.9 8.6 %gather_fusion = bf16[64,128,768]{2,1,0:T(8,128)(2,1)} fusion(bf16[8,128,768]{2,1,0:T(8,128)(2,1)} %bitcast.81, s32[1024]{0:T(1024)S(1)} %pad_clamp_fusion.1), kind=kCustom, calls=%fused_computation | custom fusion | bytes 25166080 | tf_op jit(solution)/shard_map/gather | solution.py:26
  40.6 9.1 %convolution_bitcast_fusion.1 = bf16[64,128,768]{1,2,0:T(8,128)(2,1)} fusion(bf16[64,128,768]{2,1,0:T(8,128)(2,1)} %gather_fusion, bf16[1,1,64,128,128]{4,3,2,1,0:T(8,128)(2,1)S(1)} %copy-done), kind=kOutput, calls=%fused_computation.3 | convolution fusion | flops 1610612736 | bytes 27262976 | tf_op jit(solution)/shard_map/tij,tjf->tif/dot_general | solution.py:27
  49.7 16.8 %copy.40 = bf16[64,128,768]{2,0,1:T(8,128)(2,1)} copy(bf16[64,128,768]{1,2,0:T(8,128)(2,1)} %convolution_bitcast_fusion.1) | data formatting | bytes 25165824 | tf_op jit(solution)/shard_map/tij,tjf->tif/dot_general | solution.py:27
  66.5 6.3 %convolution_convert_fusion.2 = bf16[8,128,768]{2,0,1:T(8,128)(2,1)S(1)} fusion(bf16[64,128,768]{2,0,1:T(8,128)(2,1)} %copy.40, s32[64]{0:T(128)S(1)} %get-tuple-element.8, pred[64]{0:T(512)(128)(4,1)S(1)} %iota_compare_fusion.2), kind=kOutput, calls=%fused_computation.9 | convolution fusion | flops 100664320 | bytes 14156096 | tf_op jit(solution)/shard_map/pt,tif->pif/dot_general | solution.py:33
  72.8 1.5 copy.41
  74.3 5.6 %all-to-all-start = ((bf16[8,128,768]{2,1,0:T(8,128)(2,1)}), bf16[8,128,768]{2,1,0:T(8,128)(2,1)}, u32[]{:S(2)}, u32[]{:S(2)}) async-start(bf16[8,128,768]{2,1,0:T(8,128)(2,1)} %copy.41), calls=%async_computation | async-start | bytes 3145728 | tf_op jit(solution)/shard_map/all_to_all | solution.py:36
  80.1 37.2 %all-to-all-done = bf16[8,128,768]{2,1,0:T(8,128)(2,1)} async-done(((bf16[8,128,768]{2,1,0:T(8,128)(2,1)}), bf16[8,128,768]{2,1,0:T(8,128)(2,1)}, u32[]{:S(2)}, u32[]{:S(2)}) %all-to-all-start) | async-done | bytes 1572896 | tf_op jit(solution)/shard_map/all_to_all | solution.py:36
  117.3 2.6 fusion.17
  119.8 0.5 copy.50
  120.3 3.3 %fusion.42 = (f32[1024]{0:T(1024)S(1)}, bf16[2,128,1024]{2,1,0:T(8,128)(2,1)S(1)}, bf16[2,128,1024]{2,1,0:T(8,128)(2,1)}) fusion(bf16[2,128,1024]{2,1,0:T(8,128)(2,1)S(1)} %bitcast.86, f32[1024]{0:T(1024)S(1)} %copy-done.4, bf16[2,128,768]{1,2,0:T(8,128)(2,1)S(1)} %copy.50, bf16[768,1024]{1,0:T(8,128)(2,1)} %param.13), kind=kOutput, calls=%fused_computation.63 | convolution fusion | flops 406322176 | bytes 3547136 | tf_op jit(solution)/shard_map/jrf,fh->jrh/dot_general | solution.py:45
  123.7 0.7 fusion.14
  124.3 0.7 convolution_convert_fusion.1
  125.0 1.4 copy.46
  126.5 4.4 %all-to-all-start.2 = ((bf16[8,128,768]{2,1,0:T(8,128)(2,1)}), bf16[8,128,768]{2,1,0:T(8,128)(2,1)}, u32[]{:S(2)}, u32[]{:S(2)}) async-start(bf16[8,128,768]{2,1,0:T(8,128)(2,1)} %copy.46), calls=%async_computation.2 | async-start | bytes 3145728 | tf_op jit(solution)/shard_map/all_to_all | solution.py:66
  131.0 2.2 convolution_bitcast_fusion.2
  133.3 0.2 reduce-scatter.2.cloned.1.call-start
  133.5 44.2 %all-to-all-done.2 = bf16[8,128,768]{2,1,0:T(8,128)(2,1)} async-done(((bf16[8,128,768]{2,1,0:T(8,128)(2,1)}), bf16[8,128,768]{2,1,0:T(8,128)(2,1)}, u32[]{:S(2)}, u32[]{:S(2)}) %all-to-all-start.2) | async-done | bytes 1572896 | tf_op jit(solution)/shard_map/all_to_all | solution.py:66
  177.7 8.6 %gather_fusion.1 = bf16[64,128,768]{2,1,0:T(8,128)(2,1)} fusion(bf16[8,128,768]{2,1,0:T(8,128)(2,1)} %all-to-all-done.2, s32[1024]{0:T(1024)S(1)} %pad_clamp_fusion), kind=kCustom, calls=%fused_computation.1 | custom fusion | bytes 25166080 | tf_op jit(solution)/shard_map/gather | solution.py:67
  186.4 9.3 %convolution_bitcast_fusion = bf16[64,128,768]{1,2,0:T(8,128)(2,1)} fusion(bf16[64,128,768]{2,1,0:T(8,128)(2,1)} %gather_fusion.1, bf16[1,1,64,128,128]{4,3,2,1,0:T(8,128)(2,1)S(1)} %copy-done), kind=kOutput, calls=%fused_computation.2 | convolution fusion | flops 1610612736 | bytes 27262976 | tf_op jit(solution)/shard_map/tji,tjf->tif/dot_general | solution.py:68
  195.6 16.8 %copy.48 = bf16[64,128,768]{2,0,1:T(8,128)(2,1)} copy(bf16[64,128,768]{1,2,0:T(8,128)(2,1)} %convolution_bitcast_fusion) | data formatting | bytes 25165824 | tf_op jit(solution)/shard_map/tji,tjf->tif/dot_general | solution.py:68
  212.5 6.3 %convolution_convert_fusion = bf16[8,128,768]{2,0,1:T(8,128)(2,1)S(1)} fusion(bf16[64,128,768]{2,0,1:T(8,128)(2,1)} %copy.48, s32[64]{0:T(128)S(1)} %bitcast.85, pred[64]{0:T(512)(128)(4,1)S(1)} %iota_compare_fusion.2), kind=kOutput, calls=%fused_computation.7 | convolution fusion | flops 100664320 | bytes 14156096 | tf_op jit(solution)/shard_map/kt,tif->kif/dot_general | solution.py:72
  218.8 1.5 copy.49
  220.3 38.3 %psum.15 = f32[1024]{0:T(1024)} all-reduce(f32[1024]{0:T(1024)S(1)} %get-tuple-element.4), channel_id=1, replica_groups=mesh['src'=4,'dst'=8] {'src','dst'}, use_global_device_ids=true, to_apply=%region_4.5 | all-reduce | flops 1024 | bytes 8192 | tf_op jit(solution)/shard_map/psum | solution.py:57
  258.7 31.1 %all-reduce.2.cloned.1.call-done = f32[768,1024]{1,0:T(8,128)} async-done(((f32[768,1024]{1,0:T(8,128)}), f32[768,1024]{1,0:T(8,128)}) %all-reduce.2.cloned.1.call-update) | async-done | bytes 3145744 | tf_op jit(solution)/shard_map/psum | solution.py:57
  289.7 29.9 %reduce-scatter.2.cloned.1.call-done = bf16[256,768]{1,0:T(8,128)(2,1)} async-done(((bf16[1024,768]{1,0:T(8,128)(2,1)}), bf16[256,768]{1,0:T(8,128)(2,1)}) %reduce-scatter.2.cloned.1.call-update) | async-done | bytes 393232 | tf_op jit(solution)/shard_map/reduce_scatter | solution.py:73
  319.6 4.0 %copy.63 = f32[768,1024]{1,0:T(8,128)} copy(f32[768,1024]{1,0:T(8,128)} %all-reduce.2.cloned.1.call-done) | data formatting | bytes 6291456
  (24 shorter events, 0.5 us)
Async XLA Ops:
  7.2 33.4 %copy-start = (bf16[1,1,64,128,128]{4,3,2,1,0:T(8,128)(2,1)S(1)}, bf16[1,1,64,128,128]{4,3,2,1,0:T(8,128)(2,1)}, u32[]{:S(2)}) copy-start(bf16[1,1,64,128,128]{4,3,2,1,0:T(8,128)(2,1)} %param.9) | copy-start | bytes 6291460
  7.2 24.8 %all-gather.2.cloned.1.call-start = ((), (), s32[]{:S(2)}) async-start(), calls=%async_computation.4 | async-start | bytes 1966080 | tf_op jit(solution)/shard_map/all_gather | solution.py:23
  10.0 64.2 %all-to-all-start.1 = ((s32[8,1,128]{2,1,0:T(1,128)}), s32[8,1,128]{2,1,0:T(1,128)S(1)}, u32[]{:S(2)}, u32[]{:S(2)}) async-start(s32[8,1,128]{2,1,0:T(1,128)} %broadcast_in_dim.16), calls=%async_computation.1 | async-start | bytes 8192 | tf_op jit(solution)/shard_map/all_to_all | solution.py:39
  74.3 43.0 %all-to-all-start = ((bf16[8,128,768]{2,1,0:T(8,128)(2,1)}), bf16[8,128,768]{2,1,0:T(8,128)(2,1)}, u32[]{:S(2)}, u32[]{:S(2)}) async-start(bf16[8,128,768]{2,1,0:T(8,128)(2,1)} %copy.41), calls=%async_computation | async-start | bytes 3145728 | tf_op jit(solution)/shard_map/all_to_all | solution.py:36
  79.8 40.5 %copy-start.3 = (bf16[256,1024]{1,0:T(8,128)(2,1)S(1)}, bf16[256,1024]{1,0:T(8,128)(2,1)}, u32[]{:S(2)}) copy-start(bf16[256,1024]{1,0:T(8,128)(2,1)} %param.15) | copy-start | bytes 1572868
  79.8 40.5 %copy-start.4 = (f32[1024]{0:T(1024)S(1)}, f32[1024]{0:T(1024)}, u32[]{:S(2)}) copy-start(f32[1024]{0:T(1024)} %param.14) | copy-start | bytes 12292
  120.3 3.3 %copy-start.2 = (bf16[768,1024]{1,0:T(8,128)(2,1)S(1)}, bf16[768,1024]{1,0:T(8,128)(2,1)}, u32[]{:S(2)}) copy-start(bf16[768,1024]{1,0:T(8,128)(2,1)} %param.13) | copy-start | bytes 4718596
  126.5 4.5 %copy-start.5 = (s32[1,1,64]{2,1,0:T(1,128)S(1)}, s32[1,1,64]{2,1,0:T(1,128)}, u32[]{:S(2)}) copy-start(s32[1,1,64]{2,1,0:T(1,128)} %param.11) | copy-start | bytes 772
  126.5 51.3 %all-to-all-start.2 = ((bf16[8,128,768]{2,1,0:T(8,128)(2,1)}), bf16[8,128,768]{2,1,0:T(8,128)(2,1)}, u32[]{:S(2)}, u32[]{:S(2)}) async-start(bf16[8,128,768]{2,1,0:T(8,128)(2,1)} %copy.46), calls=%async_computation.2 | async-start | bytes 3145728 | tf_op jit(solution)/shard_map/all_to_all | solution.py:66
  130.9 158.8 %all-reduce.2.cloned.1.call-start = ((), (), s32[]{:S(2)}) async-start(), calls=%async_computation.6 | async-start | bytes 6291456 | tf_op jit(solution)/shard_map/psum | solution.py:57
  133.3 186.4 %reduce-scatter.2.cloned.1.call-start = ((), (), s32[]{:S(2)}) async-start(), calls=%async_computation.5 | async-start | bytes 1966080 | tf_op jit(solution)/shard_map/reduce_scatter | solution.py:73
  195.6 16.8 %copy-start.1 = (s32[1,1,64]{2,1,0:T(1,128)S(1)}, s32[1,1,64]{2,1,0:T(1,128)}, u32[]{:S(2)}) copy-start(s32[1,1,64]{2,1,0:T(1,128)} %param.10) | copy-start | bytes 772
Sparse Core Ops, SparseCore 0:
  9.5 22.3 all-gather.1
  137.8 151.9 all-reduce.1
  292.8 26.7 reduce-scatter.1
where the time goes:
time: 331 us; the launch traced here: 330 us
  waiting for transfers between devices  157 us (47%)
  local copies, waits for them, and re-layouts  60.7 us (18%)
  matrix products  40.5 us (12%)
  blocking collectives  38.3 us (12%)
  starting transfers between devices  17.6 us (5%)
  between operations  14.5 us (4%)
    all_to_all x1, waiting for transfers between devices, per_device(): lax.all_to_all(replies, 'dst', split_axis=0, concat_axis=0, tiled=True)  44.2 us
    psum x1, blocking collectives, per_device(): weight_grad, bias_grad = lax.psum((weight_term, bias_term), ('src', 'dst'))  38.3 us
    all_to_all x1, waiting for transfers between devices, per_device(): lax.all_to_all(outgoing.astype(jnp.bfloat16), 'dst', split_axis=0, concat...  37.2 us
    psum x1, waiting for transfers between devices, per_device(): weight_grad, bias_grad = lax.psum((weight_term, bias_term), ('src', 'dst'))  31.1 us
    reduce_scatter x1, waiting for transfers between devices, per_device(): lax.psum_scatter(src_terms.reshape(holders * block_rows, feat_width).asty...  29.9 us
    dot_general x1, local copies, waits for them, and re-layouts, per_device(): jnp.einsum('tji,tjf->tif', adjacency, wanted, preferred_element_type=jnp....  16.8 us
    dot_general x1, local copies, waits for them, and re-layouts, per_device(): jnp.einsum('tij,tjf->tif', adjacency, picked, preferred_element_type=jnp....  16.8 us
    all_gather x1, waiting for transfers between devices, per_device(): lax.all_gather(features, 'src', axis=0, tiled=True)  14 us
  transfers between devices with their start and end apart: 6, of which 5 were waited for; matrix products, arithmetic and copies ran while one was open for 27% of the time, Pallas kernels for 0%

commit v1 on v0

--- a/solution.py
+++ b/solution.py
@@ -1,7 +1,16 @@
+import functools
 import jax
 import jax.numpy as jnp
 from jax import lax
 from jax.sharding import PartitionSpec as P
+
+
+def register_group(local_array, shard_axis, comm_axis):
+    a_next = lax.psum(local_array, axis_name=shard_axis)
+    return lax.psum(a_next, axis_name=comm_axis)
+
+
+_order_series_all = functools.partial(register_group, shard_axis="dst", comm_axis="src")
 
 
 def per_device(features, edge_tiles, tile_src, tile_dst, tile_count, weight, out_bias, out_grad):
@@ -54,7 +63,7 @@
         "jrf,jrh->fh", aggregate, pre_grad_b, preferred_element_type=jnp.float32
     )
     bias_term = jnp.sum(pre_grad, axis=(0, 1))
-    weight_grad, bias_grad = lax.psum((weight_term, bias_term), ("src", "dst"))
+    weight_grad, bias_grad = _order_series_all((weight_term, bias_term))
     back = jnp.einsum("jrh,fh->jrf", pre_grad_b, weight, preferred_element_type=jnp.float32).astype(
         jnp.bfloat16
     )

time: 331 us -> 398 us (1.20)
  waiting for transfers between devices: 157 us -> 234 us
  blocking collectives: 38.3 us -> 26.5 us
    psum x1 -> x2, waiting for transfers between devices: 31.1 us -> 85.6 us  [the longest x1 76.1 us: register_group(): a_next = lax.psum(local_array, axis_name=shard_axis)]
    all_to_all x1, waiting for transfers between devices: 44.2 us -> 65.4 us  [per_device(): lax.all_to_all(replies, 'dst', split_axis=0, concat_axis=0, tiled=True)]
    psum x1 -> x2, blocking collectives: 38.3 us -> 26.5 us  [the longest x1 19.5 us: register_group(): a_next = lax.psum(local_array, axis_name=shard_axis)]
  transfers between devices with their start and end apart: 6 -> 7, of which waited for: 5 -> 6; matrix products, arithmetic and copies ran while one was open for 27% -> 23% of each run, Pallas kernels for 0% -> 0%
where the time goes in v1:
time: 398 us; the launch traced here: 396 us
  waiting for transfers between devices  234 us (59%)
  local copies, waits for them, and re-layouts  60.5 us (15%)
  matrix products  41.8 us (11%)
  blocking collectives  26.5 us (7%)
  starting transfers between devices  17.6 us (4%)
  between operations  14.5 us (4%)
    psum x1, waiting for transfers between devices, register_group(): a_next = lax.psum(local_array, axis_name=shard_axis)  76.1 us
    all_to_all x1, waiting for transfers between devices, per_device(): lax.all_to_all(replies, 'dst', split_axis=0, concat_axis=0, tiled=True)  65.4 us
    all_to_all x1, waiting for transfers between devices, per_device(): lax.all_to_all(outgoing.astype(jnp.bfloat16), 'dst', split_axis=0, concat...  37.2 us
    reduce_scatter x1, waiting for transfers between devices, per_device(): lax.psum_scatter(src_terms.reshape(holders * block_rows, feat_width).asty...  31.2 us
    psum x1, blocking collectives, register_group(): a_next = lax.psum(local_array, axis_name=shard_axis)  19.5 us
    dot_general x1, local copies, waits for them, and re-layouts, per_device(): jnp.einsum('tji,tjf->tif', adjacency, wanted, preferred_element_type=jnp....  16.8 us
    dot_general x1, local copies, waits for them, and re-layouts, per_device(): jnp.einsum('tij,tjf->tif', adjacency, picked, preferred_element_type=jnp....  16.8 us
    all_gather x1, waiting for transfers between devices, per_device(): lax.all_gather(features, 'src', axis=0, tiled=True)  14 us
  transfers between devices with their start and end apart: 7, of which 6 were waited for; matrix products, arithmetic and copies ran while one was open for 23% of the time, Pallas kernels for 0%

profile of v1, /device:TPU:0, one launch (start us, length us, event | category | flops | bytes accessed | tf_op | source)
XLA Modules:
  0.0 396.5 jit_solution(8741359882224986218)
XLA Ops:
  7.2 0.7 all-gather.2.cloned.1.call-update
  8.6 0.7 and_select_fusion.1
  9.4 0.7 broadcast_in_dim.16
  10.0 7.3 %all-to-all-start.1 = ((s32[8,1,128]{2,1,0:T(1,128)}), s32[8,1,128]{2,1,0:T(1,128)S(1)}, u32[]{:S(2)}, u32[]{:S(2)}) async-start(s32[8,1,128]{2,1,0:T(1,128)} %broadcast_in_dim.16), calls=%async_computation.1 | async-start | bytes 8192 | tf_op jit(solution)/shard_map/all_to_all | solution.py:48
  17.3 0.7 fusion.39
  18.0 14.0 %all-gather.2.cloned.1.call-done = bf16[1024,768]{1,0:T(8,128)(2,1)} async-done(((bf16[256,768]{1,0:T(8,128)(2,1)}), bf16[1024,768]{1,0:T(8,128)(2,1)}) %all-gather.2.cloned.1.call-update) | async-done | bytes 1572880 | tf_op jit(solution)/shard_map/all_gather | solution.py:32
  31.9 8.7 %gather_fusion = bf16[64,128,768]{2,1,0:T(8,128)(2,1)} fusion(bf16[8,128,768]{2,1,0:T(8,128)(2,1)} %bitcast.81, s32[1024]{0:T(1024)S(1)} %pad_clamp_fusion.1), kind=kCustom, calls=%fused_computation | custom fusion | bytes 25166080 | tf_op jit(solution)/shard_map/gather | solution.py:35
  40.6 9.1 %convolution_bitcast_fusion.1 = bf16[64,128,768]{1,2,0:T(8,128)(2,1)} fusion(bf16[64,128,768]{2,1,0:T(8,128)(2,1)} %gather_fusion, bf16[1,1,64,128,128]{4,3,2,1,0:T(8,128)(2,1)S(1)} %copy-done), kind=kOutput, calls=%fused_computation.3 | convolution fusion | flops 1610612736 | bytes 27262976 | tf_op jit(solution)/shard_map/tij,tjf->tif/dot_general | solution.py:36
  49.7 16.8 %copy.40 = bf16[64,128,768]{2,0,1:T(8,128)(2,1)} copy(bf16[64,128,768]{1,2,0:T(8,128)(2,1)} %convolution_bitcast_fusion.1) | data formatting | bytes 25165824 | tf_op jit(solution)/shard_map/tij,tjf->tif/dot_general | solution.py:36
  66.5 6.3 %convolution_convert_fusion.2 = bf16[8,128,768]{2,0,1:T(8,128)(2,1)S(1)} fusion(bf16[64,128,768]{2,0,1:T(8,128)(2,1)} %copy.40, s32[64]{0:T(128)S(1)} %get-tuple-element.8, pred[64]{0:T(512)(128)(4,1)S(1)} %iota_compare_fusion.2), kind=kOutput, calls=%fused_computation.9 | convolution fusion | flops 100664320 | bytes 14156096 | tf_op jit(solution)/shard_map/pt,tif->pif/dot_general | solution.py:42
  72.8 1.5 copy.41
  74.3 5.7 %all-to-all-start = ((bf16[8,128,768]{2,1,0:T(8,128)(2,1)}), bf16[8,128,768]{2,1,0:T(8,128)(2,1)}, u32[]{:S(2)}, u32[]{:S(2)}) async-start(bf16[8,128,768]{2,1,0:T(8,128)(2,1)} %copy.41), calls=%async_computation | async-start | bytes 3145728 | tf_op jit(solution)/shard_map/all_to_all | solution.py:45
  80.2 37.2 %all-to-all-done = bf16[8,128,768]{2,1,0:T(8,128)(2,1)} async-done(((bf16[8,128,768]{2,1,0:T(8,128)(2,1)}), bf16[8,128,768]{2,1,0:T(8,128)(2,1)}, u32[]{:S(2)}, u32[]{:S(2)}) %all-to-all-start) | async-done | bytes 1572896 | tf_op jit(solution)/shard_map/all_to_all | solution.py:45
  117.4 2.6 fusion.17
  120.5 3.2 fusion.42
  123.7 2.2 convolution_bitcast_fusion.2
  125.9 2.0 fusion.14
  128.0 0.7 convolution_convert_fusion.1
  128.7 1.4 copy.46
  130.1 4.3 %all-to-all-start.2 = ((bf16[8,128,768]{2,1,0:T(8,128)(2,1)}), bf16[8,128,768]{2,1,0:T(8,128)(2,1)}, u32[]{:S(2)}, u32[]{:S(2)}) async-start(bf16[8,128,768]{2,1,0:T(8,128)(2,1)} %copy.46), calls=%async_computation.2 | async-start | bytes 3145728 | tf_op jit(solution)/shard_map/all_to_all | solution.py:75
  134.7 65.4 %all-to-all-done.2 = bf16[8,128,768]{2,1,0:T(8,128)(2,1)} async-done(((bf16[8,128,768]{2,1,0:T(8,128)(2,1)}), bf16[8,128,768]{2,1,0:T(8,128)(2,1)}, u32[]{:S(2)}, u32[]{:S(2)}) %all-to-all-start.2) | async-done | bytes 1572896 | tf_op jit(solution)/shard_map/all_to_all | solution.py:75
  200.1 8.6 %gather_fusion.1 = bf16[64,128,768]{2,1,0:T(8,128)(2,1)} fusion(bf16[8,128,768]{2,1,0:T(8,128)(2,1)} %all-to-all-done.2, s32[1024]{0:T(1024)S(1)} %pad_clamp_fusion), kind=kCustom, calls=%fused_computation.1 | custom fusion | bytes 25166080 | tf_op jit(solution)/shard_map/gather | solution.py:76
  208.6 76.1 %all-reduce.3.cloned.1.call-done = f32[768,1024]{1,0:T(8,128)} async-done(((f32[768,1024]{1,0:T(8,128)}), f32[768,1024]{1,0:T(8,128)}) %all-reduce.3.cloned.1.call-update) | async-done | bytes 3145744 | tf_op jit(solution)/shard_map/psum | solution.py:9
  284.8 9.3 %convolution_bitcast_fusion = bf16[64,128,768]{1,2,0:T(8,128)(2,1)} fusion(bf16[64,128,768]{2,1,0:T(8,128)(2,1)} %gather_fusion.1, bf16[1,1,64,128,128]{4,3,2,1,0:T(8,128)(2,1)S(1)} %copy-done), kind=kOutput, calls=%fused_computation.2 | convolution fusion | flops 1610612736 | bytes 27262976 | tf_op jit(solution)/shard_map/tji,tjf->tif/dot_general | solution.py:77
  294.1 16.8 %copy.48 = bf16[64,128,768]{2,0,1:T(8,128)(2,1)} copy(bf16[64,128,768]{1,2,0:T(8,128)(2,1)} %convolution_bitcast_fusion) | data formatting | bytes 25165824 | tf_op jit(solution)/shard_map/tji,tjf->tif/dot_general | solution.py:77
  311.0 6.4 %convolution_convert_fusion = bf16[8,128,768]{2,0,1:T(8,128)(2,1)S(1)} fusion(bf16[64,128,768]{2,0,1:T(8,128)(2,1)} %copy.48, s32[64]{0:T(128)S(1)} %bitcast.85, pred[64]{0:T(512)(128)(4,1)S(1)} %iota_compare_fusion.2), kind=kOutput, calls=%fused_computation.7 | convolution fusion | flops 100664320 | bytes 14156096 | tf_op jit(solution)/shard_map/kt,tif->kif/dot_general | solution.py:81
  317.3 1.5 copy.49
  318.8 19.5 %psum.30 = f32[1024]{0:T(1024)S(1)} all-reduce(f32[1024]{0:T(1024)S(1)} %get-tuple-element.4), channel_id=1, replica_groups=mesh['src'=4,'dst'=8] {'dst'}, use_global_device_ids=true, to_apply=%region_5.6 | all-reduce | flops 1024 | bytes 8192 | tf_op jit(solution)/shard_map/psum | solution.py:9
  338.3 7.1 %psum.31 = f32[1024]{0:T(1024)} all-reduce(f32[1024]{0:T(1024)S(1)} %psum.30), channel_id=1, replica_groups=mesh['src'=4,'dst'=8] {'src'}, use_global_device_ids=true, to_apply=%region_6.7 | all-reduce | flops 1024 | bytes 8192 | tf_op jit(solution)/shard_map/psum | solution.py:10
  345.3 9.5 %all-reduce.5.cloned.1.call-done = f32[768,1024]{1,0:T(8,128)} async-done(((f32[768,1024]{1,0:T(8,128)}), f32[768,1024]{1,0:T(8,128)}) %all-reduce.5.cloned.1.call-update) | async-done | bytes 3145744 | tf_op jit(solution)/shard_map/psum | solution.py:10
  354.8 31.2 %reduce-scatter.2.cloned.1.call-done = bf16[256,768]{1,0:T(8,128)(2,1)} async-done(((bf16[1024,768]{1,0:T(8,128)(2,1)}), bf16[256,768]{1,0:T(8,128)(2,1)}) %reduce-scatter.2.cloned.1.call-update) | async-done | bytes 393232 | tf_op jit(solution)/shard_map/reduce_scatter | solution.py:82
  386.0 4.0 %copy.64 = f32[768,1024]{1,0:T(8,128)} copy(f32[768,1024]{1,0:T(8,128)} %all-reduce.5.cloned.1.call-done) | data formatting | bytes 6291456
  (26 shorter events, 1.3 us)
Async XLA Ops:
  7.2 33.4 %copy-start = (bf16[1,1,64,128,128]{4,3,2,1,0:T(8,128)(2,1)S(1)}, bf16[1,1,64,128,128]{4,3,2,1,0:T(8,128)(2,1)}, u32[]{:S(2)}) copy-start(bf16[1,1,64,128,128]{4,3,2,1,0:T(8,128)(2,1)} %param.9) | copy-start | bytes 6291460
  7.2 24.8 %all-gather.2.cloned.1.call-start = ((), (), s32[]{:S(2)}) async-start(), calls=%async_computation.4 | async-start | bytes 1966080 | tf_op jit(solution)/shard_map/all_gather | solution.py:32
  10.0 64.2 %all-to-all-start.1 = ((s32[8,1,128]{2,1,0:T(1,128)}), s32[8,1,128]{2,1,0:T(1,128)S(1)}, u32[]{:S(2)}, u32[]{:S(2)}) async-start(s32[8,1,128]{2,1,0:T(1,128)} %broadcast_in_dim.16), calls=%async_computation.1 | async-start | bytes 8192 | tf_op jit(solution)/shard_map/all_to_all | solution.py:48
  74.3 46.2 %copy-start.2 = (bf16[256,1024]{1,0:T(8,128)(2,1)S(1)}, bf16[256,1024]{1,0:T(8,128)(2,1)}, u32[]{:S(2)}) copy-start(bf16[256,1024]{1,0:T(8,128)(2,1)} %param.15) | copy-start | bytes 1572868
  74.3 46.2 %copy-start.3 = (f32[1024]{0:T(1024)S(1)}, f32[1024]{0:T(1024)}, u32[]{:S(2)}) copy-start(f32[1024]{0:T(1024)} %param.14) | copy-start | bytes 12292
  74.3 43.1 %all-to-all-start = ((bf16[8,128,768]{2,1,0:T(8,128)(2,1)}), bf16[8,128,768]{2,1,0:T(8,128)(2,1)}, u32[]{:S(2)}, u32[]{:S(2)}) async-start(bf16[8,128,768]{2,1,0:T(8,128)(2,1)} %copy.41), calls=%async_computation | async-start | bytes 3145728 | tf_op jit(solution)/shard_map/all_to_all | solution.py:45
  80.0 204.8 %all-reduce.3.cloned.1.call-start = ((), (), s32[]{:S(2)}) async-start(), calls=%async_computation.6 | async-start | bytes 6291456 | tf_op jit(solution)/shard_map/psum | solution.py:9
  128.7 6.0 %copy-start.4 = (s32[1,1,64]{2,1,0:T(1,128)S(1)}, s32[1,1,64]{2,1,0:T(1,128)}, u32[]{:S(2)}) copy-start(s32[1,1,64]{2,1,0:T(1,128)} %param.11) | copy-start | bytes 772
  130.1 70.0 %all-to-all-start.2 = ((bf16[8,128,768]{2,1,0:T(8,128)(2,1)}), bf16[8,128,768]{2,1,0:T(8,128)(2,1)}, u32[]{:S(2)}, u32[]{:S(2)}) async-start(bf16[8,128,768]{2,1,0:T(8,128)(2,1)} %copy.46), calls=%async_computation.2 | async-start | bytes 3145728 | tf_op jit(solution)/shard_map/all_to_all | solution.py:75
  134.4 220.4 %all-reduce.5.cloned.1.call-start = ((), (), s32[]{:S(2)}) async-start(), calls=%async_computation.7 | async-start | bytes 6291456 | tf_op jit(solution)/shard_map/psum | solution.py:10
  284.8 101.2 %reduce-scatter.2.cloned.1.call-start = ((), (), s32[]{:S(2)}) async-start(), calls=%async_computation.5 | async-start | bytes 1966080 | tf_op jit(solution)/shard_map/reduce_scatter | solution.py:82
  294.1 16.8 %copy-start.1 = (s32[1,1,64]{2,1,0:T(1,128)S(1)}, s32[1,1,64]{2,1,0:T(1,128)}, u32[]{:S(2)}) copy-start(s32[1,1,64]{2,1,0:T(1,128)} %param.10) | copy-start | bytes 772
Sparse Core Ops, SparseCore 0:
  9.5 22.3 all-gather.1
  126.0 158.6 all-reduce.2
  287.1 67.6 all-reduce.4
  357.8 28.1 reduce-scatter.1
